TPU v7x, 32 devices: a whole 2x2x4 slice. The times are simulated.
32 devices in a mesh: dp: 8 (over y, x, core), tensor: 4 (over z).
Axes of the slice: x: 2, y: 2, z: 4, core: 2. Of those that a mesh axis runs over, the one named last changes fastest.
Arguments:
- frames: bfloat16 [2, 8, 1152, 1024], P(None, 'dp'), may hold values from -6 to 6
- skip_frames: bfloat16 [2, 8, 1152, 1024], P(None, 'dp'), may hold values from -6 to 6
- cotangent: bfloat16 [2, 8, 1152, 1024], P(None, 'dp'), may hold values from -6 to 6
- lengths: int32 [2, 8], P(None, 'dp'), may hold values from 288 to 1152, as said below
- time_steps: int32 [2, 8], P(None, 'dp'), may hold values from 0 to 63
- time_table: bfloat16 [64, 1024], replicated, may hold values from -6 to 6
- w_skip: bfloat16 [2048, 1024], replicated, may hold values from -0.125 to 0.125
- w_gamma_attn: bfloat16 [1024, 1024], replicated, may hold values from -0.1875 to 0.1875
- w_gamma_ffn: bfloat16 [1024, 1024], replicated, may hold values from -0.1875 to 0.1875
- w_qkv: bfloat16 [3, 1024, 1024], P(None, None, 'tensor'), may hold values from -0.1875 to 0.1875
- w_out: bfloat16 [1024, 1024], P('tensor'), may hold values from -0.75 to 0.75
- w_up: bfloat16 [1024, 4096], P(None, 'tensor'), may hold values from -0.1875 to 0.1875
- b_up: bfloat16 [4096], P('tensor'), may hold values from -4 to 4
- w_down: bfloat16 [4096, 1024], P('tensor'), may hold values from -0.09375 to 0.09375
Outputs:
- mixed: bfloat16 [2, 8, 1152, 1024], P(None, 'dp')
- grad_frames: bfloat16 [2, 8, 1152, 1024], P(None, 'dp')
- grad_skip: bfloat16 [2, 8, 1152, 1024], P(None, 'dp')
- grad_table: float32 [64, 1024], P('dp')
- grad_w_skip: float32 [2048, 1024], P(('dp', 'tensor'))
- grad_w_gamma_attn: float32 [1024, 1024], P('dp')
- grad_w_gamma_ffn: float32 [1024, 1024], P('dp')
- grad_w_qkv: float32 [3, 1024, 1024], P(None, 'dp', 'tensor')
- grad_w_out: float32 [1024, 1024], P('tensor', 'dp')
- grad_w_up: float32 [1024, 4096], P('dp', 'tensor')
- grad_b_up: float32 [4096], P('tensor')
- grad_w_down: float32 [4096, 1024], P('tensor', 'dp')
Inputs may be any that keep to these rules, and one draw needn't show every extreme that they name: `lengths`: the live frames of an utterance are its first slots; in every micro-batch one utterance fills all 1152 slots.
All inputs are finite; a program needn't handle non-finite values.
Results may differ from a plain program's by a relative error of at most 0.025.
The roundings to bfloat16 on the way count: a program that leaves them out, or rounds other values in their place, can miss the bound.
Values may be sent and summed in bfloat16 or wider, within the bound.
No kernel may reach another device: no remote copies, remote signals or barrier semaphores. Data moves between devices by JAX's collectives and lax.ppermute only.
A program may use at most 256 MiB of HBM per device.

v0:
```python
import math
import jax
import jax.numpy as jnp
from jax import lax
from jax.sharding import PartitionSpec as P

HD = 64
EPSILON = 1e-06
MASKED = -1e30


def rope_tables(length, head_size):
    half_size = head_size // 2
    places = jnp.arange(length, dtype=jnp.float32)
    frequency = jnp.exp(
        jnp.arange(half_size, dtype=jnp.float32) * (-2.0 * math.log(10000.0) / head_size)
    )
    angles = places[:, None] * frequency[None, :]
    return (jnp.cos(angles)[:, None, :], jnp.sin(angles)[:, None, :])


def rotate(values, cosine, sine):
    half_size = values.shape[-1] // 2
    front_half = values[..., :half_size]
    back_half = values[..., half_size:]
    return jnp.concatenate(
        [front_half * cosine - back_half * sine, back_half * cosine + front_half * sine], axis=-1
    )


def unrotate(gradient, cosine, sine):
    half_size = gradient.shape[-1] // 2
    front_half = gradient[..., :half_size]
    back_half = gradient[..., half_size:]
    return jnp.concatenate(
        [front_half * cosine + back_half * sine, back_half * cosine - front_half * sine], axis=-1
    )


def normalize(hidden):
    factor = lax.rsqrt(jnp.mean(hidden * hidden, axis=-1, keepdims=True) + EPSILON)
    return (hidden * factor, factor)


def norm_back(grad_normed, normed, factor):
    return factor * (grad_normed - normed * jnp.mean(grad_normed * normed, axis=-1, keepdims=True))


def scores_of(queries, keys_rot, live_keys, score_scale):
    raw_scores = (
        jnp.einsum("slhe,smhe->shlm", queries, keys_rot, preferred_element_type=jnp.float32)
        * score_scale
    )
    return jnp.where(live_keys[:, None, None, :], raw_scores, MASKED)


def gelu_exact(values):
    return jax.nn.gelu(values, approximate=False)


def local(
    frames,
    skip_frames,
    cotangent,
    lengths,
    time_steps,
    time_table,
    w_skip,
    w_gamma_attn,
    w_gamma_ffn,
    w_qkv,
    w_out,
    w_up,
    b_up,
    w_down,
):
    micro_count, seq_count, length, model_width = frames.shape
    local_width = w_qkv.shape[2]
    heads_local = local_width // HD
    row_count = seq_count * length
    table_rows = time_table.shape[0]
    score_scale = 1.0 / math.sqrt(HD)
    cosine, sine = rope_tables(length, HD)
    places = jnp.arange(length)
    bias_f32 = b_up.astype(jnp.float32)
    grad_w_down = jnp.zeros(w_down.shape, jnp.float32)
    grad_w_up = jnp.zeros(w_up.shape, jnp.float32)
    grad_b_up = jnp.zeros(b_up.shape, jnp.float32)
    grad_w_out = jnp.zeros(w_out.shape, jnp.float32)
    grad_w_qkv = jnp.zeros(w_qkv.shape, jnp.float32)
    grad_w_skip = jnp.zeros(w_skip.shape, jnp.float32)
    grad_gamma_attn = jnp.zeros(w_gamma_attn.shape, jnp.float32)
    grad_gamma_ffn = jnp.zeros(w_gamma_ffn.shape, jnp.float32)
    grad_table = jnp.zeros(time_table.shape, jnp.float32)
    mixed_list = []
    frame_grads = []
    skip_grads_list = []
    for micro_index in range(micro_count):
        live_keys = places[None, :] < lengths[micro_index][:, None]
        live_rows = live_keys.astype(jnp.float32)[:, :, None]
        onehot = time_steps[micro_index][:, None] == jnp.arange(table_rows)[None, :]
        condition = jnp.dot(
            onehot.astype(jnp.bfloat16), time_table, preferred_element_type=jnp.float32
        ).astype(jnp.bfloat16)
        gain_attn = 1.0 + jnp.dot(condition, w_gamma_attn, preferred_element_type=jnp.float32)
        gain_ffn = 1.0 + jnp.dot(condition, w_gamma_ffn, preferred_element_type=jnp.float32)
        joined = jnp.concatenate([frames[micro_index], skip_frames[micro_index]], axis=-1).reshape(
            row_count, 2 * model_width
        )
        skip_mixed = jnp.dot(joined, w_skip, preferred_element_type=jnp.float32).reshape(
            seq_count, length, model_width
        )
        normed_one, factor_one = normalize(skip_mixed)
        attn_in = (
            (normed_one * gain_attn[:, None, :])
            .astype(jnp.bfloat16)
            .reshape(row_count, model_width)
        )
        projected = jnp.einsum("rd,cde->cre", attn_in, w_qkv, preferred_element_type=jnp.float32)
        projected = projected.reshape(3, seq_count, length, heads_local, HD)
        queries = rotate(projected[0], cosine, sine).astype(jnp.bfloat16)
        keys_rot = rotate(projected[1], cosine, sine).astype(jnp.bfloat16)
        values = projected[2].astype(jnp.bfloat16)
        raw_scores = scores_of(queries, keys_rot, live_keys, score_scale)
        maxima = jnp.max(raw_scores, axis=-1, keepdims=True)
        logsum = maxima + jnp.log(jnp.sum(jnp.exp(raw_scores - maxima), axis=-1, keepdims=True))
        weights_low = jnp.exp(raw_scores - logsum).astype(jnp.bfloat16)
        context = jnp.einsum(
            "shlm,smhe->slhe", weights_low, values, preferred_element_type=jnp.float32
        ).astype(jnp.bfloat16)
        context = context.reshape(row_count, local_width)
        attn_total = lax.psum(
            jnp.dot(context, w_out, preferred_element_type=jnp.float32).astype(jnp.bfloat16),
            "tensor",
        ).astype(jnp.float32)
        middle = skip_mixed + attn_total.reshape(seq_count, length, model_width)
        normed_two, factor_two = normalize(middle)
        ffn_in = (
            (normed_two * gain_ffn[:, None, :]).astype(jnp.bfloat16).reshape(row_count, model_width)
        )
        pre_act = jnp.dot(ffn_in, w_up, preferred_element_type=jnp.float32) + bias_f32[None, :]
        activated = gelu_exact(pre_act).astype(jnp.bfloat16)
        ffn_total = lax.psum(
            jnp.dot(activated, w_down, preferred_element_type=jnp.float32).astype(jnp.bfloat16),
            "tensor",
        ).astype(jnp.float32)
        result = (middle + ffn_total.reshape(seq_count, length, model_width)) * live_rows
        mixed_list.append(result.astype(jnp.bfloat16))
        grad_low = (cotangent[micro_index] * live_rows.astype(jnp.bfloat16)).reshape(
            row_count, model_width
        )
        grad_out = grad_low.astype(jnp.float32).reshape(seq_count, length, model_width)
        grad_w_down = grad_w_down + jnp.dot(
            activated.T, grad_low, preferred_element_type=jnp.float32
        )
        grad_act = jnp.dot(grad_low, w_down.T, preferred_element_type=jnp.float32)
        _, gelu_back = jax.vjp(gelu_exact, pre_act)
        grad_pre = gelu_back(grad_act)[0].astype(jnp.bfloat16)
        grad_b_up = grad_b_up + jnp.sum(grad_pre.astype(jnp.float32), axis=0)
        grad_w_up = grad_w_up + jnp.dot(ffn_in.T, grad_pre, preferred_element_type=jnp.float32)
        grad_ffn_in = lax.psum(
            jnp.dot(grad_pre, w_up.T, preferred_element_type=jnp.float32).astype(jnp.bfloat16),
            "tensor",
        ).astype(jnp.float32)
        grad_ffn_in = grad_ffn_in.reshape(seq_count, length, model_width)
        gain_ffn_low = jnp.sum(grad_ffn_in * normed_two, axis=1).astype(jnp.bfloat16)
        grad_middle = grad_out + norm_back(
            grad_ffn_in * gain_ffn[:, None, :], normed_two, factor_two
        )
        grad_attn = grad_middle.astype(jnp.bfloat16).reshape(row_count, model_width)
        grad_w_out = grad_w_out + jnp.dot(context.T, grad_attn, preferred_element_type=jnp.float32)
        grad_context = jnp.dot(grad_attn, w_out.T, preferred_element_type=jnp.float32).astype(
            jnp.bfloat16
        )
        grad_context = grad_context.reshape(seq_count, length, heads_local, HD)
        grad_values = jnp.einsum(
            "shlm,slhe->smhe", weights_low, grad_context, preferred_element_type=jnp.float32
        ).astype(jnp.bfloat16)
        grad_probs = jnp.einsum(
            "slhe,smhe->shlm", grad_context, values, preferred_element_type=jnp.float32
        )
        probs = jnp.exp(scores_of(queries, keys_rot, live_keys, score_scale) - logsum)
        inner_sum = jnp.sum(probs * grad_probs, axis=-1, keepdims=True)
        grad_scores = (probs * (grad_probs - inner_sum)).astype(jnp.bfloat16)
        grad_queries = (
            jnp.einsum("shlm,smhe->slhe", grad_scores, keys_rot, preferred_element_type=jnp.float32)
            * score_scale
        )
        grad_keys = (
            jnp.einsum("shlm,slhe->smhe", grad_scores, queries, preferred_element_type=jnp.float32)
            * score_scale
        )
        grad_proj = jnp.stack(
            [
                unrotate(grad_queries, cosine, sine).astype(jnp.bfloat16),
                unrotate(grad_keys, cosine, sine).astype(jnp.bfloat16),
                grad_values,
            ]
        ).reshape(3, row_count, local_width)
        grad_w_qkv = grad_w_qkv + jnp.einsum(
            "rd,cre->cde", attn_in, grad_proj, preferred_element_type=jnp.float32
        )
        grad_attn_in = lax.psum(
            jnp.einsum("cre,cde->rd", grad_proj, w_qkv, preferred_element_type=jnp.float32).astype(
                jnp.bfloat16
            ),
            "tensor",
        ).astype(jnp.float32)
        grad_attn_in = grad_attn_in.reshape(seq_count, length, model_width)
        gain_attn_low = jnp.sum(grad_attn_in * normed_one, axis=1).astype(jnp.bfloat16)
        grad_base = grad_middle + norm_back(
            grad_attn_in * gain_attn[:, None, :], normed_one, factor_one
        )
        grad_base = grad_base.astype(jnp.bfloat16).reshape(row_count, model_width)
        grad_joined = jnp.dot(grad_base, w_skip.T, preferred_element_type=jnp.float32).reshape(
            seq_count, length, 2 * model_width
        )
        frame_grads.append(grad_joined[..., :model_width].astype(jnp.bfloat16))
        skip_grads_list.append(grad_joined[..., model_width:].astype(jnp.bfloat16))
        grad_w_skip = grad_w_skip + jnp.dot(joined.T, grad_base, preferred_element_type=jnp.float32)
        grad_gamma_attn = grad_gamma_attn + jnp.dot(
            condition.T, gain_attn_low, preferred_element_type=jnp.float32
        )
        grad_gamma_ffn = grad_gamma_ffn + jnp.dot(
            condition.T, gain_ffn_low, preferred_element_type=jnp.float32
        )
        grad_condition = jnp.dot(
            gain_attn_low, w_gamma_attn.T, preferred_element_type=jnp.float32
        ) + jnp.dot(gain_ffn_low, w_gamma_ffn.T, preferred_element_type=jnp.float32)
        grad_table = grad_table + jnp.dot(
            onehot.astype(jnp.float32).T, grad_condition, precision=lax.Precision.HIGHEST
        )
    bias_grad = lax.psum(grad_b_up, "dp")
    summed = (
        lax.psum_scatter(
            grad_w_qkv.astype(jnp.bfloat16), "dp", scatter_dimension=1, tiled=True
        ).astype(jnp.float32),
        lax.psum_scatter(
            grad_w_out.astype(jnp.bfloat16), "dp", scatter_dimension=1, tiled=True
        ).astype(jnp.float32),
        lax.psum_scatter(
            grad_w_up.astype(jnp.bfloat16), "dp", scatter_dimension=0, tiled=True
        ).astype(jnp.float32),
        lax.psum_scatter(
            grad_w_down.astype(jnp.bfloat16), "dp", scatter_dimension=1, tiled=True
        ).astype(jnp.float32),
        lax.psum_scatter(
            grad_gamma_attn.astype(jnp.bfloat16), "dp", scatter_dimension=0, tiled=True
        ).astype(jnp.float32),
        lax.psum_scatter(
            grad_gamma_ffn.astype(jnp.bfloat16), "dp", scatter_dimension=0, tiled=True
        ).astype(jnp.float32),
        lax.psum_scatter(
            grad_table.astype(jnp.bfloat16), "dp", scatter_dimension=0, tiled=True
        ).astype(jnp.float32),
        lax.psum_scatter(
            grad_w_skip.astype(jnp.bfloat16), "dp", scatter_dimension=0, tiled=True
        ).astype(jnp.float32),
    )
    share_rows = summed[7].shape[0] // lax.axis_size("tensor")
    skip_total = lax.dynamic_slice_in_dim(
        summed[7], lax.axis_index("tensor") * share_rows, share_rows, 0
    )
    return (
        jnp.stack(mixed_list),
        jnp.stack(frame_grads),
        jnp.stack(skip_grads_list),
        summed[6],
        skip_total,
        summed[4],
        summed[5],
        summed[0],
        summed[1],
        summed[2],
        bias_grad,
        summed[3],
    )


def solution(mesh):
    placed = (
        P(None, "dp", None, None),
        P(None, "dp", None, None),
        P(None, "dp", None, None),
        P(None, "dp"),
        P(None, "dp"),
        P(),
        P(),
        P(),
        P(),
        P(None, None, "tensor"),
        P("tensor", None),
        P(None, "tensor"),
        P("tensor"),
        P("tensor", None),
    )
    return jax.shard_map(
        local,
        mesh=mesh,
        in_specs=placed,
        out_specs=(
            P(None, "dp", None, None),
            P(None, "dp", None, None),
            P(None, "dp", None, None),
            P("dp", None),
            P(("dp", "tensor"), None),
            P("dp", None),
            P("dp", None),
            P(None, "dp", "tensor"),
            P("tensor", "dp"),
            P("dp", "tensor"),
            P("tensor"),
            P("tensor", "dp"),
        ),
        check_vma=False,
    )
```

profile of v0, /device:TPU:0, one launch (start us, length us, event | category | flops | bytes accessed | tf_op | source)
XLA Modules:
  0.0 1307.0 jit_solution(4355509511752099064)
XLA Ops:
  12.9 4.4 slice_bitcast_fusion.6
  17.9 5.9 multiply_reduce_fusion.5
  29.8 6.2 multiply_reduce_fusion.3
  47.1 12.8 exponential_reduce_fusion
  71.2 10.5 fusion.65
  84.0 10.5 fusion.59
  97.7 5.1 fusion.140
  107.2 4.7 copy.130
  113.9 158.6 %all-reduce.11.cloned.1.call-done = (bf16[1152,1024]{0,1:T(8,128)(2,1)}, bf16[1152,1024]{0,1:T(8,128)(2,1)}) async-done(((bf16[1152,1024]{0,1:T(8,128)(2,1)}, bf16[1152,1024]{0,1:T(8,128)(2,1)}), (bf16[1152,1024]{0,1:T(8,128)(2,1)}, bf16[1152,1024]{0,1:T(8,128)(2,1)})) %all-reduce.11.cloned.1.call-update) | async-done | bytes 4718608 | tf_op jit(solution)/shard_map/psum | solution.py:132
  278.5 14.3 %multiply_convert_fusion.3 = (bf16[1152,1024]{1,0:T(8,128)(2,1)}, f32[1152,1024]{1,0:T(8,128)S(1)}, f32[1152,1024]{1,0:T(8,128)S(1)}) fusion(f32[1024]{0:T(1024)S(1)} %convert_element_type.428, bf16[1024,1024]{1,0:T(8,128)(2,1)S(1)} %copy-done, f32[1152,1024]{0,1:T(8,128)S(1)} %get-tuple-element.63, f32[1024]{0:T(1024)S(1)} %get-tuple-element.142, ...), kind=kOutput, calls=%fused_computation.69 | convolution fusion | flops 2497314816 | bytes 18625024 | tf_op jit(solution)/shard_map/dot_general | solution.py:141
  292.9 5.1 convert_reduce_fusion
  302.1 14.4 %multiply_convert_fusion.7 = (bf16[1152,1024]{1,0:T(8,128)(2,1)}, f32[1152,1024]{1,0:T(8,128)S(1)}, f32[1152,1024]{1,0:T(8,128)S(1)}) fusion(f32[1024]{0:T(1024)S(1)} %convert_element_type.428, bf16[1024,1024]{1,0:T(8,128)(2,1)S(1)} %copy-done, f32[1152,1024]{0,1:T(8,128)S(1)} %get-tuple-element.59, f32[1024]{0:T(1024)S(1)} %broadcast_add_fusion.2, ...), kind=kOutput, calls=%fused_computation.88 | convolution fusion | flops 2497314816 | bytes 18625024 | tf_op jit(solution)/shard_map/dot_general | solution.py:141
  316.6 5.1 convert_reduce_fusion.1
  328.8 6.0 convolution_convert_fusion.4
  334.8 4.4 convolution_convert_fusion.6
  339.2 159.1 %all-reduce.9.cloned.1.call-done = (bf16[1152,1024]{0,1:T(8,128)(2,1)}, bf16[1152,1024]{0,1:T(8,128)(2,1)}) async-done(((bf16[1152,1024]{0,1:T(8,128)(2,1)}, bf16[1152,1024]{0,1:T(8,128)(2,1)}), (bf16[1152,1024]{0,1:T(8,128)(2,1)}, bf16[1152,1024]{0,1:T(8,128)(2,1)})) %all-reduce.9.cloned.1.call-update) | async-done | bytes 4718608 | tf_op jit(solution)/shard_map/psum | solution.py:161
  498.3 5.1 fusion.28
  509.6 11.3 fusion.62
  520.9 13.3 %multiply_reduce_fusion.1 = (f32[4,1152]{1,0:T(4,128)S(1)}, f32[4,1152,1152]{1,2,0:T(8,128)}) fusion(f32[4,1152,1152]{1,2,0:T(8,128)} %copy-done.3, f32[4,1152]{1,0:T(4,128)S(1)} %copy-done.67, bf16[1152,4,64]{0,2,1:T(8,128)(2,1)S(1)} %bitcast.283, bf16[1152,4,64]{0,2,1:T(8,128)(2,1)S(1)} %bitcast.274), kind=kOutput, calls=%fused_computation.7 | convolution fusion | flops 695397888 | bytes 43683840 | tf_op jit(solution)/shard_map/slhe,smhe->shlm/dot_general | solution.py:179
  534.2 14.4 %multiply_convert_fusion.1 = bf16[4,1152,1152]{1,2,0:T(8,128)(2,1)S(1)} fusion(f32[4,1152,1152]{1,2,0:T(8,128)} %get-tuple-element.129, f32[4,1152,1152]{1,2,0:T(8,128)} %copy-done.3, f32[4,1152]{1,0:T(4,128)S(1)} %get-tuple-element.128, f32[4,1152]{1,0:T(4,128)S(1)} %copy-done.67), kind=kLoop, calls=%fused_computation.6 | loop fusion | flops 21233664 | bytes 53121024 | tf_op jit(solution)/shard_map/convert_element_type | solution.py:184
  559.4 11.4 fusion.68
  570.8 13.4 %multiply_reduce_fusion = (f32[4,1152]{1,0:T(4,128)S(1)}, f32[4,1152,1152]{1,2,0:T(8,128)}) fusion(f32[4,1152,1152]{1,2,0:T(8,128)} %copy-done.2, f32[4,1152]{1,0:T(4,128)S(1)} %copy-done.65, bf16[1152,4,64]{0,2,1:T(8,128)(2,1)S(1)} %bitcast.285, bf16[1152,4,64]{0,2,1:T(8,128)(2,1)S(1)} %bitcast.276), kind=kOutput, calls=%fused_computation.5 | convolution fusion | flops 695397888 | bytes 43683840 | tf_op jit(solution)/shard_map/slhe,smhe->shlm/dot_general | solution.py:179
  584.2 14.4 %multiply_convert_fusion = bf16[4,1152,1152]{1,2,0:T(8,128)(2,1)S(1)} fusion(f32[4,1152,1152]{1,2,0:T(8,128)} %get-tuple-element.131, f32[4,1152,1152]{1,2,0:T(8,128)} %copy-done.2, f32[4,1152]{1,0:T(4,128)S(1)} %get-tuple-element.130, f32[4,1152]{1,0:T(4,128)S(1)} %copy-done.65), kind=kLoop, calls=%fused_computation.4 | loop fusion | flops 21233664 | bytes 53121024 | tf_op jit(solution)/shard_map/convert_element_type | solution.py:184
  598.6 4.4 fusion.58
  618.2 5.4 bitcast_convert_fusion
  627.8 5.4 fusion.75
  639.1 5.8 fusion.135
  645.0 6.7 add_convert_fusion.4
  659.6 4.9 fusion.86
  664.6 5.9 fusion.78
  670.5 4.3 copy.124
  679.3 271.8 %all-reduce.7.cloned.1.call-done = (bf16[1152,1024]{0,1:T(8,128)(2,1)}, bf16[1152,1024]{0,1:T(8,128)(2,1)}, bf16[1152,1024]{0,1:T(8,128)(2,1)}, bf16[1152,1024]{0,1:T(8,128)(2,1)}) async-done(((bf16[1152,1024]{0,1:T(8,128)(2,1)}, bf16[1152,1024]{0,1:T(8,128)(2,1)}, bf16[1152,1024]{0,1:T(8,128)(2,1)}, bf16[1152,1024]{0,1:T(8,128)(2,1)}), (bf16[1152,1024]{0,1:T(8,128)(2,1)}, bf16[1152,1024]{0,1:T(8,128)(2,1)}, ...) | async-done | bytes 9437200 | tf_op jit(solution)/shard_map/psum | solution.py:143
  951.1 4.6 fusion.31
  966.2 9.5 fusion.24
  975.7 8.2 fusion.45
  984.0 9.8 fusion.17
  996.2 7.7 add_convert_fusion
  1003.9 14.4 %psum.71 = f32[1024]{0:T(1024)} all-reduce(f32[1024]{0:T(1024)S(1)} %add.246), channel_id=1, replica_groups=mesh['dp'=8,'tensor'=4] {'dp'}, use_global_device_ids=true, to_apply=%region_35.36 | all-reduce | flops 1024 | bytes 8192 | tf_op jit(solution)/shard_map/psum | solution.py:233
  1020.3 18.4 %reduce-scatter.23.cloned.1.call-done = bf16[128,1024]{1,0:T(8,128)(2,1)} async-done(((bf16[1024,1024]{1,0:T(8,128)(2,1)}), bf16[128,1024]{1,0:T(8,128)(2,1)}) %reduce-scatter.23.cloned.1.call-update) | async-done | bytes 262160 | tf_op jit(solution)/shard_map/reduce_scatter | solution.py:241
  1040.4 35.9 %reduce-scatter.27.cloned.1.call-done = bf16[128,256]{1,0:T(8,128)(2,1)} async-done(((bf16[1024,256]{1,0:T(8,128)(2,1)}), bf16[128,256]{1,0:T(8,128)(2,1)}) %reduce-scatter.27.cloned.1.call-update) | async-done | bytes 65552
  1078.0 40.0 %reduce-scatter.25.cloned.1.call-done = bf16[128,768]{1,0:T(8,128)(2,1)} async-done(((bf16[1024,768]{1,0:T(8,128)(2,1)}), bf16[128,768]{1,0:T(8,128)(2,1)}) %reduce-scatter.25.cloned.1.call-update) | async-done | bytes 196624
  1120.1 5.0 pad_maximum_fusion
  1125.1 6.6 copy.92
  1131.8 7.7 fusion.5
  1142.4 5.3 fusion.4
  1156.5 43.1 %reduce-scatter.19.cloned.1.call-done = bf16[128,1024]{1,0:T(8,128)(2,1)} async-done(((bf16[1024,1024]{1,0:T(8,128)(2,1)}), bf16[128,1024]{1,0:T(8,128)(2,1)}) %reduce-scatter.19.cloned.1.call-update) | async-done | bytes 262160 | tf_op jit(solution)/shard_map/reduce_scatter | solution.py:247
  1201.4 42.5 %reduce-scatter.21.cloned.1.call-done = bf16[128,1024]{1,0:T(8,128)(2,1)} async-done(((bf16[1024,1024]{1,0:T(8,128)(2,1)}), bf16[128,1024]{1,0:T(8,128)(2,1)}) %reduce-scatter.21.cloned.1.call-update) | async-done | bytes 262160 | tf_op jit(solution)/shard_map/reduce_scatter | solution.py:250
  1245.6 52.7 %reduce-scatter.17.cloned.1.call-done = bf16[256,1024]{1,0:T(8,128)(2,1)} async-done(((bf16[2048,1024]{1,0:T(8,128)(2,1)}), bf16[256,1024]{1,0:T(8,128)(2,1)}) %reduce-scatter.17.cloned.1.call-update) | async-done | bytes 524304 | tf_op jit(solution)/shard_map/reduce_scatter | solution.py:256
  (364 shorter events, 154.6 us)
Async XLA Ops:
  7.2 271.3 %copy-start = (bf16[1024,1024]{1,0:T(8,128)(2,1)S(1)}, bf16[1024,1024]{1,0:T(8,128)(2,1)}, u32[]{:S(2)}) copy-start(bf16[1024,1024]{1,0:T(8,128)(2,1)} %param.25) | copy-start | bytes 6291460
  7.2 265.3 %all-reduce.11.cloned.1.call-start = ((), (), s32[]{:S(2)}) async-start(), calls=%async_computation.18 | async-start | bytes 9437184 | tf_op jit(solution)/shard_map/psum | solution.py:132
  12.9 11.0 copy-start.86
  17.3 12.5 copy-start.46
  17.3 12.5 copy-start.48
  26.4 57.7 %copy-start.26 = (bf16[1,1152,256]{1,2,0:T(8,128)(2,1)}, bf16[1,1152,256]{1,2,0:T(8,128)(2,1)S(1)}, u32[]{:S(2)}) copy-start(bf16[1,1152,256]{1,2,0:T(8,128)(2,1)S(1)} %slice.289) | copy-start | bytes 1769476
  38.6 32.5 %copy-start.28 = (bf16[1,1152,256]{1,2,0:T(8,128)(2,1)}, bf16[1,1152,256]{1,2,0:T(8,128)(2,1)S(1)}, u32[]{:S(2)}) copy-start(bf16[1,1152,256]{1,2,0:T(8,128)(2,1)S(1)} %slice.288) | copy-start | bytes 1769476
  43.0 16.9 %copy-start.38 = (bf16[1152,4,32]{0,2,1:T(8,128)(2,1)}, bf16[1152,4,32]{0,2,1:T(8,128)(2,1)S(1)}, u32[]{:S(2)}) copy-start(bf16[1152,4,32]{0,2,1:T(8,128)(2,1)S(1)} %get-tuple-element.104) | copy-start | bytes 884740
  43.0 16.9 %copy-start.40 = (bf16[1152,4,32]{0,2,1:T(8,128)(2,1)}, bf16[1152,4,32]{0,2,1:T(8,128)(2,1)S(1)}, u32[]{:S(2)}) copy-start(bf16[1152,4,32]{0,2,1:T(8,128)(2,1)S(1)} %get-tuple-element.105) | copy-start | bytes 884740
  43.0 16.9 %copy-start.42 = (bf16[1152,4,32]{0,2,1:T(8,128)(2,1)}, bf16[1152,4,32]{0,2,1:T(8,128)(2,1)S(1)}, u32[]{:S(2)}) copy-start(bf16[1152,4,32]{0,2,1:T(8,128)(2,1)S(1)} %get-tuple-element.108) | copy-start | bytes 884740
  43.0 16.9 %copy-start.44 = (bf16[1152,4,32]{0,2,1:T(8,128)(2,1)}, bf16[1152,4,32]{0,2,1:T(8,128)(2,1)S(1)}, u32[]{:S(2)}) copy-start(bf16[1152,4,32]{0,2,1:T(8,128)(2,1)S(1)} %get-tuple-element.109) | copy-start | bytes 884740
  47.1 12.8 copy-start.2
  59.9 11.2 copy-start.64
  71.1 12.9 copy-start.66
  71.2 10.5 copy-start.58
  81.7 12.8 copy-start.22
  97.7 400.6 %all-reduce.9.cloned.1.call-start = ((), (), s32[]{:S(2)}) async-start(), calls=%async_computation.17 | async-start | bytes 9437184 | tf_op jit(solution)/shard_map/psum | solution.py:161
  111.9 164.6 %slice-start.2 = ((s8[4718592]{0:T(1024)(128)(4,1)}), s8[524288]{0:T(1024)(128)(4,1)S(1)}, s32[]{:S(2)}) async-start(s8[4718592]{0:T(1024)(128)(4,1)} %bitcast.265), calls=%async_computation.21 | async-start | bytes 1048576
  276.5 25.6 %copy-start.5 = (f32[1152,1024]{0,1:T(8,128)}, f32[1152,1024]{0,1:T(8,128)S(1)}, u32[]{:S(2)}) copy-start(f32[1152,1024]{0,1:T(8,128)S(1)} %get-tuple-element.59) | copy-start | bytes 14155780
  278.5 14.4 %copy-start.4 = (f32[1152,1024]{0,1:T(8,128)}, f32[1152,1024]{0,1:T(8,128)S(1)}, u32[]{:S(2)}) copy-start(f32[1152,1024]{0,1:T(8,128)S(1)} %get-tuple-element.63) | copy-start | bytes 14155780
  278.5 14.4 %copy-start.14 = (bf16[1,1,1152,1024]{2,3,1,0:T(8,128)(2,1)S(1)}, bf16[1,1,1152,1024]{2,3,1,0:T(8,128)(2,1)}, u32[]{:S(2)}) copy-start(bf16[1,1,1152,1024]{2,3,1,0:T(8,128)(2,1)} %copy.131) | copy-start | bytes 7077892
  278.5 14.4 %copy-start.100 = (bf16[1024,1024]{1,0:T(8,128)(2,1)S(1)}, bf16[1024,1024]{1,0:T(8,128)(2,1)}, u32[]{:S(2)}) copy-start(bf16[1024,1024]{1,0:T(8,128)(2,1)} %param.27) | copy-start | bytes 6291460
  302.1 14.4 %copy-start.17 = (bf16[1,1,1152,1024]{2,3,1,0:T(8,128)(2,1)S(1)}, bf16[1,1,1152,1024]{2,3,1,0:T(8,128)(2,1)}, u32[]{:S(2)}) copy-start(bf16[1,1,1152,1024]{2,3,1,0:T(8,128)(2,1)} %copy.130) | copy-start | bytes 7077892
  302.1 14.4 %copy-start.90 = (bf16[1152]{0:T(1024)(128)(2,1)S(1)}, bf16[1152]{0:T(1024)(128)(2,1)}, u32[]{:S(2)}) copy-start(bf16[1152]{0:T(1024)(128)(2,1)} %get-tuple-element.139) | copy-start | bytes 6916
  327.2 623.9 %all-reduce.7.cloned.1.call-start = ((), (), s32[]{:S(2)}) async-start(), calls=%async_computation.16 | async-start | bytes 18874368 | tf_op jit(solution)/shard_map/psum | solution.py:143
  509.6 11.4 copy-start.27
  534.2 14.4 %copy-start.43 = (bf16[1152,4,32]{0,2,1:T(8,128)(2,1)S(1)}, bf16[1152,4,32]{0,2,1:T(8,128)(2,1)}, u32[]{:S(2)}) copy-start(bf16[1152,4,32]{0,2,1:T(8,128)(2,1)} %copy-done.42) | copy-start | bytes 884740
  534.2 14.4 %copy-start.45 = (bf16[1152,4,32]{0,2,1:T(8,128)(2,1)S(1)}, bf16[1152,4,32]{0,2,1:T(8,128)(2,1)}, u32[]{:S(2)}) copy-start(bf16[1152,4,32]{0,2,1:T(8,128)(2,1)} %copy-done.44) | copy-start | bytes 884740
  559.4 11.4 copy-start.29
  584.2 14.4 %copy-start.35 = (bf16[1152,4,32]{0,2,1:T(8,128)(2,1)S(1)}, bf16[1152,4,32]{0,2,1:T(8,128)(2,1)}, u32[]{:S(2)}) copy-start(bf16[1152,4,32]{0,2,1:T(8,128)(2,1)} %copy-done.34) | copy-start | bytes 884740
  584.2 14.4 %copy-start.37 = (bf16[1152,4,32]{0,2,1:T(8,128)(2,1)S(1)}, bf16[1152,4,32]{0,2,1:T(8,128)(2,1)}, u32[]{:S(2)}) copy-start(bf16[1152,4,32]{0,2,1:T(8,128)(2,1)} %copy-done.36) | copy-start | bytes 884740
  627.3 391.0 %reduce-scatter.29.cloned.1.call-start = ((), (), s32[]{:S(2)}) async-start(), calls=%async_computation.15 | async-start | bytes 2359296
  639.1 399.6 %reduce-scatter.23.cloned.1.call-start = ((), (), s32[]{:S(2)}) async-start(), calls=%async_computation.12 | async-start | bytes 2359296 | tf_op jit(solution)/shard_map/reduce_scatter | solution.py:241
  645.0 8.0 copy-start.25
  651.7 424.6 %reduce-scatter.27.cloned.1.call-start = ((), (), s32[]{:S(2)}) async-start(), calls=%async_computation.14 | async-start | bytes 589824
  659.3 458.7 %reduce-scatter.25.cloned.1.call-start = ((), (), s32[]{:S(2)}) async-start(), calls=%async_computation.13 | async-start | bytes 1769472
  677.9 477.2 %reduce-scatter.15.cloned.1.call-start = ((), (), s32[]{:S(2)}) async-start(), calls=%async_computation.8 | async-start | bytes 147456 | tf_op jit(solution)/shard_map/reduce_scatter | solution.py:253
  961.8 237.8 %reduce-scatter.19.cloned.1.call-start = ((), (), s32[]{:S(2)}) async-start(), calls=%async_computation.10 | async-start | bytes 2359296 | tf_op jit(solution)/shard_map/reduce_scatter | solution.py:247
  964.6 279.3 %reduce-scatter.21.cloned.1.call-start = ((), (), s32[]{:S(2)}) async-start(), calls=%async_computation.11 | async-start | bytes 2359296 | tf_op jit(solution)/shard_map/reduce_scatter | solution.py:250
  966.2 9.5 copy-start.51
  966.2 9.5 copy-start.53
  975.7 8.2 copy-start.55
  983.9 314.5 %reduce-scatter.17.cloned.1.call-start = ((), (), s32[]{:S(2)}) async-start(), calls=%async_computation.9 | async-start | bytes 4718592 | tf_op jit(solution)/shard_map/reduce_scatter | solution.py:256
  984.0 11.2 copy-start.47
  984.0 11.2 copy-start.49
  984.0 12.2 copy-start.109
  996.2 7.7 copy-start.95
  1150.9 149.2 %copy-start.1 = (bf16[1024,1024]{1,0:T(8,128)(2,1)S(1)}, bf16[1024,1024]{1,0:T(8,128)(2,1)}, u32[]{:S(2)}) copy-start(bf16[1024,1024]{1,0:T(8,128)(2,1)} %param.25) | copy-start | bytes 6291460
  (77 other events, 323.5 us)
Sparse Core Ops, SparseCore 0:
  97.8 174.6 all-reduce.10
  327.3 170.9 all-reduce.8
  627.4 323.6 all-reduce.6
  954.2 40.0 reduce-scatter.28
  997.5 41.1 reduce-scatter.22
  1042.2 34.1 reduce-scatter.26
  1079.6 38.3 reduce-scatter.24
  1121.5 33.5 reduce-scatter.14
  1158.5 41.0 reduce-scatter.18
  1202.7 41.0 reduce-scatter.20
  1247.2 51.1 reduce-scatter.16
where the time goes:
time: 1320 us; the launch traced here: 1310 us
  waiting for transfers between devices  824 us (62%)
  matrix products  257 us (19%)
  other arithmetic  124 us (9%)
  local copies, waits for them, and re-layouts  70.4 us (5%)
  between operations  16 us (1%)
  blocking collectives  14.4 us (1%)
    psum x1, waiting for transfers between devices, local(): lax.psum(jnp.dot(activated, w_down, preferred_element_type=jnp.float32).a...  272 us
    psum x1, waiting for transfers between devices, local(): lax.psum(jnp.dot(grad_pre, w_up.T, preferred_element_type=jnp.float32).as...  159 us
    psum x1, waiting for transfers between devices, local(): lax.psum(jnp.dot(context, w_out, preferred_element_type=jnp.float32).asty...  159 us
    unnamed x14, waiting for transfers between devices  76.1 us
    reduce_scatter x1, waiting for transfers between devices, local(): lax.psum_scatter(grad_w_skip.astype(jnp.bfloat16), 'dp', scatter_dimensio...  52.7 us
    unnamed x240, local copies, waits for them, and re-layouts  49.6 us
    reduce_scatter x1, waiting for transfers between devices, local(): lax.psum_scatter(grad_gamma_attn.astype(jnp.bfloat16), 'dp', scatter_dime...  43.1 us
    reduce_scatter x1, waiting for transfers between devices, local(): lax.psum_scatter(grad_gamma_ffn.astype(jnp.bfloat16), 'dp', scatter_dimen...  42.5 us
  transfers between devices with their start and end apart: 11, of which 10 were waited for; matrix products, arithmetic and copies ran while one was open for 13% of the time, Pallas kernels for 0%

commit v1 on v0

--- a/solution.py
+++ b/solution.py
@@ -158,9 +158,12 @@
         grad_pre = gelu_back(grad_act)[0].astype(jnp.bfloat16)
         grad_b_up = grad_b_up + jnp.sum(grad_pre.astype(jnp.float32), axis=0)
         grad_w_up = grad_w_up + jnp.dot(ffn_in.T, grad_pre, preferred_element_type=jnp.float32)
-        grad_ffn_in = lax.psum(
-            jnp.dot(grad_pre, w_up.T, preferred_element_type=jnp.float32).astype(jnp.bfloat16),
-            "tensor",
+        grad_ffn_in = jnp.sum(
+            lax.all_gather(
+                jnp.dot(grad_pre, w_up.T, preferred_element_type=jnp.float32).astype(jnp.bfloat16),
+                "tensor",
+            ),
+            axis=0,
         ).astype(jnp.float32)
         grad_ffn_in = grad_ffn_in.reshape(seq_count, length, model_width)
         gain_ffn_low = jnp.sum(grad_ffn_in * normed_two, axis=1).astype(jnp.bfloat16)

time: 1320 us -> 1410 us (1.068)
  waiting for transfers between devices: 824 us -> 885 us
  other arithmetic: 124 us -> 141 us
    all_gather x0 -> x2, waiting for transfers between devices: none -> 216 us  [local(): lax.all_gather(jnp.dot(grad_pre, w_up.T, preferred_element_type=jnp.float...]
    psum x1 -> x0, waiting for transfers between devices: 159 us -> none  [local(): lax.psum(jnp.dot(grad_pre, w_up.T, preferred_element_type=jnp.float32).as...]
    reduce_sum x0 -> x2, other arithmetic: none -> 16.4 us  [local(): jnp.sum(lax.all_gather(jnp.dot(grad_pre, w_up.T, preferred_element_type=j...]
    unnamed x240 -> x232, local copies, waits for them, and re-layouts: 49.6 us -> 51.6 us
    unnamed x14 -> x15, waiting for transfers between devices: 76.1 us -> 76.2 us
  transfers between devices with their start and end apart: 11 -> 12, of which waited for: 10 -> 11; matrix products, arithmetic and copies ran while one was open for 13% -> 19% of each run, Pallas kernels for 0% -> 0%
where the time goes in v1:
time: 1410 us; the launch traced here: 1400 us
  waiting for transfers between devices  885 us (63%)
  matrix products  260 us (18%)
  other arithmetic  141 us (10%)
  local copies, waits for them, and re-layouts  81.4 us (6%)
  between operations  16.3 us (1%)
  blocking collectives  14.1 us (1%)
    psum x1, waiting for transfers between devices, local(): lax.psum(jnp.dot(activated, w_down, preferred_element_type=jnp.float32).a...  271 us
    all_gather x2, waiting for transfers between devices, local(): lax.all_gather(jnp.dot(grad_pre, w_up.T, preferred_element_type=jnp.float...  216 us
    psum x1, waiting for transfers between devices, local(): lax.psum(jnp.dot(context, w_out, preferred_element_type=jnp.float32).asty...  163 us
    unnamed x15, waiting for transfers between devices  76.2 us
    reduce_scatter x1, waiting for transfers between devices, local(): lax.psum_scatter(grad_w_skip.astype(jnp.bfloat16), 'dp', scatter_dimensio...  52.6 us
    unnamed x232, local copies, waits for them, and re-layouts  51.6 us
    reduce_scatter x1, waiting for transfers between devices, local(): lax.psum_scatter(grad_gamma_attn.astype(jnp.bfloat16), 'dp', scatter_dime...  42.9 us
    reduce_scatter x1, waiting for transfers between devices, local(): lax.psum_scatter(grad_gamma_ffn.astype(jnp.bfloat16), 'dp', scatter_dimen...  42.6 us
  transfers between devices with their start and end apart: 12, of which 11 were waited for; matrix products, arithmetic and copies ran while one was open for 19% of the time, Pallas kernels for 0%

profile of v1, /device:TPU:0, one launch (start us, length us, event | category | flops | bytes accessed | tf_op | source)
XLA Modules:
  0.0 1398.5 jit_solution(14919963843692695515)
XLA Ops:
  17.8 5.9 multiply_reduce_fusion.5
  29.9 6.1 multiply_reduce_fusion.3
  65.3 10.5 fusion.65
  78.2 10.5 fusion.59
  91.9 5.2 fusion.140
  103.5 163.2 %all-reduce.7.cloned.1.call-done = (bf16[1152,1024]{0,1:T(8,128)(2,1)}, bf16[1152,1024]{0,1:T(8,128)(2,1)}) async-done(((bf16[1152,1024]{0,1:T(8,128)(2,1)}, bf16[1152,1024]{0,1:T(8,128)(2,1)}), (bf16[1152,1024]{0,1:T(8,128)(2,1)}, bf16[1152,1024]{0,1:T(8,128)(2,1)})) %all-reduce.7.cloned.1.call-update) | async-done | bytes 4718608 | tf_op jit(solution)/shard_map/psum | solution.py:132
  270.6 14.4 %multiply_convert_fusion.7 = (bf16[1152,1024]{1,0:T(8,128)(2,1)}, f32[1152,1024]{1,0:T(8,128)S(1)}, f32[1152,1024]{1,0:T(8,128)S(1)}) fusion(f32[1024]{0:T(1024)S(1)} %convert_element_type.432, bf16[1024,1024]{1,0:T(8,128)(2,1)S(1)} %copy-done, f32[1152,1024]{0,1:T(8,128)S(1)} %get-tuple-element.57, f32[1024]{0:T(1024)S(1)} %broadcast_add_fusion.2, ...), kind=kOutput, calls=%fused_computation.88 | convolution fusion | flops 2497314816 | bytes 18625024 | tf_op jit(solution)/shard_map/dot_general | solution.py:141
  285.0 5.1 convert_reduce_fusion.1
  299.9 4.8 multiply_reduce_fusion.2
  304.7 14.2 %multiply_convert_fusion.3 = (bf16[1152,1024]{1,0:T(8,128)(2,1)}, f32[1152,1024]{1,0:T(8,128)S(1)}, f32[1152,1024]{1,0:T(8,128)S(1)}) fusion(f32[1024]{0:T(1024)S(1)} %convert_element_type.432, bf16[1024,1024]{1,0:T(8,128)(2,1)S(1)} %copy-done, f32[1152,1024]{0,1:T(8,128)S(1)} %get-tuple-element.61, f32[1024]{0:T(1024)S(1)} %get-tuple-element.140, ...), kind=kOutput, calls=%fused_computation.69 | convolution fusion | flops 2497314816 | bytes 18625024 | tf_op jit(solution)/shard_map/dot_general | solution.py:141
  319.0 5.1 convert_reduce_fusion
  329.5 6.9 convolution_convert_fusion.4
  336.5 6.1 convolution_convert_fusion.6
  342.6 118.8 %all-gather.5.cloned.1.call-done = bf16[4608,1024]{1,0:T(8,128)(2,1)} async-done(((bf16[1152,1024]{1,0:T(8,128)(2,1)}), bf16[4608,1024]{1,0:T(8,128)(2,1)}) %all-gather.5.cloned.1.call-update) | async-done | bytes 9437200 | tf_op jit(solution)/shard_map/all_gather | solution.py:162
  461.4 8.2 reduce_sum.192
  474.1 5.3 fusion.28
  485.8 13.6 multiply_reduce_fusion.1
  499.4 15.0 %multiply_convert_fusion.1 = bf16[4,1152,1152]{1,2,0:T(8,128)(2,1)S(1)} fusion(f32[4,1152,1152]{1,2,0:T(8,128)} %get-tuple-element.127, f32[4,1152,1152]{1,2,0:T(8,128)} %copy-done.3, f32[4,1152]{1,0:T(4,128)S(1)} %get-tuple-element.126, f32[4,1152]{1,0:T(4,128)S(1)} %copy-done.67), kind=kLoop, calls=%fused_computation.6 | loop fusion | flops 21233664 | bytes 53121024 | tf_op jit(solution)/shard_map/convert_element_type | solution.py:187
  519.5 11.4 fusion.62
  530.9 97.0 %all-gather.7.cloned.1.call-done = bf16[4608,1024]{1,0:T(8,128)(2,1)} async-done(((bf16[1152,1024]{1,0:T(8,128)(2,1)}), bf16[4608,1024]{1,0:T(8,128)(2,1)}) %all-gather.7.cloned.1.call-update) | async-done | bytes 9437200 | tf_op jit(solution)/shard_map/all_gather | solution.py:162
  627.9 8.2 reduce_sum.196
  640.6 4.6 fusion.30
  651.4 11.4 fusion.68
  662.8 13.2 multiply_reduce_fusion
  676.0 14.6 %multiply_convert_fusion = bf16[4,1152,1152]{1,2,0:T(8,128)(2,1)S(1)} fusion(f32[4,1152,1152]{1,2,0:T(8,128)} %get-tuple-element.129, f32[4,1152,1152]{1,2,0:T(8,128)} %copy-done.2, f32[4,1152]{1,0:T(4,128)S(1)} %get-tuple-element.128, f32[4,1152]{1,0:T(4,128)S(1)} %copy-done.65), kind=kLoop, calls=%fused_computation.4 | loop fusion | flops 21233664 | bytes 53121024 | tf_op jit(solution)/shard_map/convert_element_type | solution.py:187
  710.2 5.4 bitcast_convert_fusion
  719.4 5.4 fusion.75
  731.1 5.8 fusion.135
  737.0 6.7 add_convert_fusion.4
  751.4 4.9 fusion.86
  756.4 5.9 fusion.78
  771.2 271.1 %all-reduce.5.cloned.1.call-done = (bf16[1152,1024]{0,1:T(8,128)(2,1)}, bf16[1152,1024]{0,1:T(8,128)(2,1)}, bf16[1152,1024]{0,1:T(8,128)(2,1)}, bf16[1152,1024]{0,1:T(8,128)(2,1)}) async-done(((bf16[1152,1024]{0,1:T(8,128)(2,1)}, bf16[1152,1024]{0,1:T(8,128)(2,1)}, bf16[1152,1024]{0,1:T(8,128)(2,1)}, bf16[1152,1024]{0,1:T(8,128)(2,1)}), (bf16[1152,1024]{0,1:T(8,128)(2,1)}, bf16[1152,1024]{0,1:T(8,128)(2,1)}, ...) | async-done | bytes 9437200 | tf_op jit(solution)/shard_map/psum | solution.py:143
  1042.3 4.6 fusion.31
  1057.1 9.5 fusion.24
  1066.6 8.2 fusion.45
  1075.1 9.8 fusion.17
  1087.3 7.7 add_convert_fusion
  1095.1 14.1 %psum.55 = f32[1024]{0:T(1024)} all-reduce(f32[1024]{0:T(1024)S(1)} %add.242), channel_id=1, replica_groups=mesh['dp'=8,'tensor'=4] {'dp'}, use_global_device_ids=true, to_apply=%region_35.36 | all-reduce | flops 1024 | bytes 8192 | tf_op jit(solution)/shard_map/psum | solution.py:236
  1111.3 18.6 %reduce-scatter.23.cloned.1.call-done = bf16[128,1024]{1,0:T(8,128)(2,1)} async-done(((bf16[1024,1024]{1,0:T(8,128)(2,1)}), bf16[128,1024]{1,0:T(8,128)(2,1)}) %reduce-scatter.23.cloned.1.call-update) | async-done | bytes 262160 | tf_op jit(solution)/shard_map/reduce_scatter | solution.py:244
  1131.7 36.0 %reduce-scatter.27.cloned.1.call-done = bf16[128,256]{1,0:T(8,128)(2,1)} async-done(((bf16[1024,256]{1,0:T(8,128)(2,1)}), bf16[128,256]{1,0:T(8,128)(2,1)}) %reduce-scatter.27.cloned.1.call-update) | async-done | bytes 65552
  1169.3 40.0 %reduce-scatter.25.cloned.1.call-done = bf16[128,768]{1,0:T(8,128)(2,1)} async-done(((bf16[1024,768]{1,0:T(8,128)(2,1)}), bf16[128,768]{1,0:T(8,128)(2,1)}) %reduce-scatter.25.cloned.1.call-update) | async-done | bytes 196624
  1211.5 5.0 pad_maximum_fusion
  1216.5 6.6 copy.90
  1223.1 7.7 fusion.5
  1233.8 5.3 fusion.4
  1247.9 42.9 %reduce-scatter.19.cloned.1.call-done = bf16[128,1024]{1,0:T(8,128)(2,1)} async-done(((bf16[1024,1024]{1,0:T(8,128)(2,1)}), bf16[128,1024]{1,0:T(8,128)(2,1)}) %reduce-scatter.19.cloned.1.call-update) | async-done | bytes 262160 | tf_op jit(solution)/shard_map/reduce_scatter | solution.py:250
  1292.6 42.6 %reduce-scatter.21.cloned.1.call-done = bf16[128,1024]{1,0:T(8,128)(2,1)} async-done(((bf16[1024,1024]{1,0:T(8,128)(2,1)}), bf16[128,1024]{1,0:T(8,128)(2,1)}) %reduce-scatter.21.cloned.1.call-update) | async-done | bytes 262160 | tf_op jit(solution)/shard_map/reduce_scatter | solution.py:253
  1337.0 52.6 %reduce-scatter.17.cloned.1.call-done = bf16[256,1024]{1,0:T(8,128)(2,1)} async-done(((bf16[2048,1024]{1,0:T(8,128)(2,1)}), bf16[256,1024]{1,0:T(8,128)(2,1)}) %reduce-scatter.17.cloned.1.call-update) | async-done | bytes 524304 | tf_op jit(solution)/shard_map/reduce_scatter | solution.py:259
  (361 shorter events, 186.3 us)
Async XLA Ops:
  7.2 263.4 %copy-start = (bf16[1024,1024]{1,0:T(8,128)(2,1)S(1)}, bf16[1024,1024]{1,0:T(8,128)(2,1)}, u32[]{:S(2)}) copy-start(bf16[1024,1024]{1,0:T(8,128)(2,1)} %param.25) | copy-start | bytes 6291460
  7.2 259.5 %all-reduce.7.cloned.1.call-start = ((), (), s32[]{:S(2)}) async-start(), calls=%async_computation.19 | async-start | bytes 9437184 | tf_op jit(solution)/shard_map/psum | solution.py:132
  12.8 11.0 copy-start.86
  17.3 12.6 copy-start.46
  17.3 12.6 copy-start.48
  26.4 51.8 %copy-start.28 = (bf16[1,1152,256]{1,2,0:T(8,128)(2,1)}, bf16[1,1152,256]{1,2,0:T(8,128)(2,1)S(1)}, u32[]{:S(2)}) copy-start(bf16[1,1152,256]{1,2,0:T(8,128)(2,1)S(1)} %slice.289) | copy-start | bytes 1769476
  38.6 26.6 %copy-start.26 = (bf16[1,1152,256]{1,2,0:T(8,128)(2,1)}, bf16[1,1152,256]{1,2,0:T(8,128)(2,1)S(1)}, u32[]{:S(2)}) copy-start(bf16[1,1152,256]{1,2,0:T(8,128)(2,1)S(1)} %slice.288) | copy-start | bytes 1769476
  42.9 11.2 copy-start.38
  42.9 11.2 copy-start.40
  42.9 11.2 copy-start.42
  42.9 11.2 copy-start.44
  54.1 11.2 copy-start.64
  65.3 12.9 copy-start.66
  65.3 10.5 copy-start.57
  75.8 12.8 copy-start.22
  91.8 369.6 %all-gather.5.cloned.1.call-start = ((), (), s32[]{:S(2)}) async-start(), calls=%async_computation.13 | async-start | bytes 11796480 | tf_op jit(solution)/shard_map/all_gather | solution.py:162
  270.5 14.5 %copy-start.5 = (f32[1152,1024]{0,1:T(8,128)}, f32[1152,1024]{0,1:T(8,128)S(1)}, u32[]{:S(2)}) copy-start(f32[1152,1024]{0,1:T(8,128)S(1)} %get-tuple-element.57) | copy-start | bytes 14155780
  270.6 14.5 %copy-start.14 = (bf16[1,1,1152,1024]{2,3,1,0:T(8,128)(2,1)S(1)}, bf16[1,1,1152,1024]{2,3,1,0:T(8,128)(2,1)}, u32[]{:S(2)}) copy-start(bf16[1,1,1152,1024]{2,3,1,0:T(8,128)(2,1)} %copy.126) | copy-start | bytes 7077892
  270.6 14.5 %copy-start.100 = (bf16[1024,1024]{1,0:T(8,128)(2,1)S(1)}, bf16[1024,1024]{1,0:T(8,128)(2,1)}, u32[]{:S(2)}) copy-start(bf16[1024,1024]{1,0:T(8,128)(2,1)} %param.27) | copy-start | bytes 6291460
  295.5 332.4 %all-gather.7.cloned.1.call-start = ((), (), s32[]{:S(2)}) async-start(), calls=%async_computation.14 | async-start | bytes 11796480 | tf_op jit(solution)/shard_map/all_gather | solution.py:162
  304.7 14.3 %copy-start.4 = (f32[1152,1024]{0,1:T(8,128)}, f32[1152,1024]{0,1:T(8,128)S(1)}, u32[]{:S(2)}) copy-start(f32[1152,1024]{0,1:T(8,128)S(1)} %get-tuple-element.61) | copy-start | bytes 14155780
  304.7 14.3 %copy-start.16 = (bf16[1,1,1152,1024]{2,3,1,0:T(8,128)(2,1)S(1)}, bf16[1,1,1152,1024]{2,3,1,0:T(8,128)(2,1)}, u32[]{:S(2)}) copy-start(bf16[1,1,1152,1024]{2,3,1,0:T(8,128)(2,1)} %copy.127) | copy-start | bytes 7077892
  304.7 14.3 %copy-start.90 = (bf16[1152]{0:T(1024)(128)(2,1)S(1)}, bf16[1152]{0:T(1024)(128)(2,1)}, u32[]{:S(2)}) copy-start(bf16[1152]{0:T(1024)(128)(2,1)} %get-tuple-element.139) | copy-start | bytes 6916
  304.7 14.3 %copy-start.101 = (bf16[1024,1024]{1,0:T(8,128)(2,1)S(1)}, bf16[1024,1024]{1,0:T(8,128)(2,1)}, u32[]{:S(2)}) copy-start(bf16[1024,1024]{1,0:T(8,128)(2,1)} %param.27) | copy-start | bytes 6291460
  336.4 705.9 %all-reduce.5.cloned.1.call-start = ((), (), s32[]{:S(2)}) async-start(), calls=%async_computation.18 | async-start | bytes 18874368 | tf_op jit(solution)/shard_map/psum | solution.py:143
  499.3 15.0 %copy-start.43 = (bf16[1152,4,32]{0,2,1:T(8,128)(2,1)S(1)}, bf16[1152,4,32]{0,2,1:T(8,128)(2,1)}, u32[]{:S(2)}) copy-start(bf16[1152,4,32]{0,2,1:T(8,128)(2,1)} %copy-done.42) | copy-start | bytes 884740
  499.4 15.0 %copy-start.45 = (bf16[1152,4,32]{0,2,1:T(8,128)(2,1)S(1)}, bf16[1152,4,32]{0,2,1:T(8,128)(2,1)}, u32[]{:S(2)}) copy-start(bf16[1152,4,32]{0,2,1:T(8,128)(2,1)} %copy-done.44) | copy-start | bytes 884740
  651.4 11.4 copy-start.27
  676.0 14.6 %copy-start.35 = (bf16[1152,4,32]{0,2,1:T(8,128)(2,1)S(1)}, bf16[1152,4,32]{0,2,1:T(8,128)(2,1)}, u32[]{:S(2)}) copy-start(bf16[1152,4,32]{0,2,1:T(8,128)(2,1)} %copy-done.34) | copy-start | bytes 884740
  676.0 14.6 %copy-start.37 = (bf16[1152,4,32]{0,2,1:T(8,128)(2,1)S(1)}, bf16[1152,4,32]{0,2,1:T(8,128)(2,1)}, u32[]{:S(2)}) copy-start(bf16[1152,4,32]{0,2,1:T(8,128)(2,1)} %copy-done.36) | copy-start | bytes 884740
  719.3 389.9 %reduce-scatter.29.cloned.1.call-start = ((), (), s32[]{:S(2)}) async-start(), calls=%async_computation.17 | async-start | bytes 2359296
  731.1 398.8 %reduce-scatter.23.cloned.1.call-start = ((), (), s32[]{:S(2)}) async-start(), calls=%async_computation.12 | async-start | bytes 2359296 | tf_op jit(solution)/shard_map/reduce_scatter | solution.py:244
  737.0 8.0 copy-start.25
  743.7 424.0 %reduce-scatter.27.cloned.1.call-start = ((), (), s32[]{:S(2)}) async-start(), calls=%async_computation.16 | async-start | bytes 589824
  751.3 458.1 %reduce-scatter.25.cloned.1.call-start = ((), (), s32[]{:S(2)}) async-start(), calls=%async_computation.15 | async-start | bytes 1769472
  769.7 476.8 %reduce-scatter.15.cloned.1.call-start = ((), (), s32[]{:S(2)}) async-start(), calls=%async_computation.8 | async-start | bytes 147456 | tf_op jit(solution)/shard_map/reduce_scatter | solution.py:256
  1053.0 237.8 %reduce-scatter.19.cloned.1.call-start = ((), (), s32[]{:S(2)}) async-start(), calls=%async_computation.10 | async-start | bytes 2359296 | tf_op jit(solution)/shard_map/reduce_scatter | solution.py:250
  1055.8 279.4 %reduce-scatter.21.cloned.1.call-start = ((), (), s32[]{:S(2)}) async-start(), calls=%async_computation.11 | async-start | bytes 2359296 | tf_op jit(solution)/shard_map/reduce_scatter | solution.py:253
  1057.1 9.5 copy-start.51
  1057.1 9.5 copy-start.53
  1066.6 8.2 copy-start.54
  1074.8 314.8 %reduce-scatter.17.cloned.1.call-start = ((), (), s32[]{:S(2)}) async-start(), calls=%async_computation.9 | async-start | bytes 4718592 | tf_op jit(solution)/shard_map/reduce_scatter | solution.py:259
  1075.1 11.3 copy-start.47
  1075.1 11.2 copy-start.49
  1075.1 12.2 copy-start.109
  1087.3 7.7 copy-start.94
  1087.3 7.8 copy-start.95
  1242.2 149.0 %copy-start.1 = (bf16[1024,1024]{1,0:T(8,128)(2,1)S(1)}, bf16[1024,1024]{1,0:T(8,128)(2,1)}, u32[]{:S(2)}) copy-start(bf16[1024,1024]{1,0:T(8,128)(2,1)} %param.25) | copy-start | bytes 6291460
  (74 other events, 323.5 us)
Sparse Core Ops, SparseCore 0:
  91.9 174.7 all-reduce.6
  295.6 165.7 all-gather.4
  463.0 164.9 all-gather.6
  719.4 322.8 all-reduce.4
  1045.5 40.0 reduce-scatter.28
  1088.7 41.1 reduce-scatter.22
  1133.5 34.1 reduce-scatter.26
  1171.0 38.3 reduce-scatter.24
  1212.9 33.5 reduce-scatter.14
  1249.7 41.0 reduce-scatter.18
  1294.1 41.0 reduce-scatter.20
  1338.4 51.1 reduce-scatter.16
